TPU v7x, 32 devices: a whole 2x2x4 slice. The times are simulated.
32 devices in a mesh: dp: 4 (over y, x), shard: 8 (over z, core).
Axes of the slice: x: 2, y: 2, z: 4, core: 2. Of those that a mesh axis runs over, the one named last changes fastest.
Arguments:
- layer_input: bfloat16 [384, 46240], P('shard', 'dp'), may hold values from -6 to 6
- cotangent: bfloat16 [32768, 512], P('dp'), may hold values from -0.032958984 to 0.032958984
- momentum: float32 [10368, 512], P('shard'), may hold values from -6 to 6
Outputs:
- momentum_new: float32 [10368, 512], P('shard')
- direction: float32 [10368, 512], P('shard')
All inputs are finite; a program needn't handle non-finite values.
Results may differ from a plain program's by a relative error of at most 0.0003.
Values sent between devices are 32-bit elements; how exact they have to be, the bound alone decides.
No kernel may reach another device: no remote copies, remote signals or barrier semaphores. Data moves between devices by JAX's collectives and lax.ppermute only.
A program may use at most 320 MiB of HBM per device.

v0:
```python
import jax
import jax.numpy as jnp
from jax import lax
from jax.sharding import PartitionSpec as P

HW = 32
ITERS = 2
ROWS = 10368
HIGH = lax.Precision.HIGHEST


def gram_sum(block):
    local = lax.dot_general(block, block, (((0,), (0,)), ((), ())), precision=HIGH)
    return lax.psum(local, "shard")


def body(layer_input, cotangent, momentum):
    chans = layer_input.shape[0]
    voxels = cotangent.shape[0]
    depth = voxels // (HW * HW)
    volume = layer_input.reshape(chans, depth + 2, HW + 2, HW + 2)
    slabs = []
    for kd in range(3):
        for kh in range(3):
            for kw in range(3):
                slabs.append(volume[:, kd : kd + depth, kh : kh + HW, kw : kw + HW])
    patches = jnp.stack(slabs, axis=1).reshape(chans * 27, voxels)
    partial_grad = jnp.dot(patches, cotangent, preferred_element_type=jnp.float32)
    grad = lax.psum(partial_grad, "dp")
    momentum_new = 0.95 * momentum + grad
    squared = lax.psum(jnp.sum(momentum_new * momentum_new), "shard")
    iterate = momentum_new / (jnp.sqrt(squared) + 1e-07)
    gram = gram_sum(iterate)
    for step in range(ITERS):
        if step > 0:
            gram = gram_sum(iterate)
        poly = -4.775 * gram + 2.0315 * jnp.dot(gram, gram, precision=HIGH)
        iterate = 3.4445 * iterate + jnp.dot(iterate, poly, precision=HIGH)
    direction = iterate * jnp.sqrt(jnp.float32(ROWS))
    return (momentum_new, direction)


def solution(mesh):
    return jax.shard_map(
        body,
        mesh=mesh,
        in_specs=(P("shard", "dp"), P("dp", None), P("shard", None)),
        out_specs=(P("shard", None), P("shard", None)),
        check_vma=False,
    )
```

profile of v0, /device:TPU:0, one launch (start us, length us, event | category | flops | bytes accessed | tf_op | source)
XLA Modules:
  0.0 549.4 jit_solution(15928005073139925350)
XLA Ops:
  7.2 8.9 %reshape.10 = bf16[48,10,34,34]{3,2,1,0:T(8,128)(2,1)} reshape(bf16[48,11560]{1,0:T(8,128)(2,1)} %param.3) | data formatting | bytes 2219520 | tf_op jit(solution)/shard_map/reshape | solution.py:21
  16.1 4.7 fusion.27
  29.5 3.9 fusion.23
  33.4 3.9 fusion.22
  37.3 3.5 fusion.21
  40.8 4.0 fusion.20
  44.9 4.0 fusion.19
  56.7 3.5 fusion.15
  60.2 3.9 fusion.14
  64.1 4.2 fusion.13
  71.7 3.8 fusion.11
  75.6 3.9 fusion.10
  87.1 3.5 fusion.6
  90.6 4.3 fusion.5
  94.9 3.8 fusion.4
  98.8 3.5 fusion.3
  102.3 4.0 fusion.2
  106.3 3.9 fusion.1
  110.2 56.4 %copy.5 = bf16[48,27,8,32,32]{4,3,2,1,0:T(8,128)(2,1)} copy(bf16[48,27,8,32,32]{4,3,2,0,1:T(8,128)(2,1)} %fusion.1) | data formatting | bytes 42467328 | tf_op jit(solution)/shard_map/stack | solution.py:27
  166.5 102.6 %reshape.11 = bf16[1296,8192]{1,0:T(8,128)(2,1)} reshape(bf16[48,27,8,32,32]{4,3,2,1,0:T(8,128)(2,1)} %copy.5) | data formatting | bytes 42467328 | tf_op jit(solution)/shard_map/reshape | solution.py:27
  269.1 19.1 %fusion.31 = f32[1296,512]{1,0:T(8,128)} fusion(bf16[1296,8192]{1,0:T(8,128)(2,1)} %reshape.11, bf16[8192,512]{1,0:T(8,128)(2,1)} %param.4), kind=kOutput, calls=%fused_computation.65 | convolution fusion | flops 10871635968 | bytes 32276480 | tf_op jit(solution)/shard_map/dot_general | solution.py:28
  288.3 81.9 %all-reduce.4.cloned.1.call-done = f32[1296,512]{1,0:T(8,128)} async-done(((f32[1296,512]{1,0:T(8,128)}), f32[1296,512]{1,0:T(8,128)}) %all-reduce.4.cloned.1.call-update) | async-done | bytes 2654224 | tf_op jit(solution)/shard_map/psum | solution.py:29
  370.2 4.5 multiply_reduce_fusion
  374.7 17.0 %psum.29 = f32[]{:T(128)} all-reduce(f32[]{:T(128)} %get-tuple-element.2), channel_id=1, replica_groups=mesh['dp'=4,'shard'=8] {'shard'}, use_global_device_ids=true, to_apply=%region_2.0 | all-reduce | flops 1 | bytes 8 | tf_op jit(solution)/shard_map/psum | solution.py:31
  392.4 8.8 %fusion.30 = f32[512,512]{1,0:T(8,128)} fusion(f32[1296,512]{1,0:T(8,128)} %get-tuple-element.3, f32[]{:T(128)S(6)} %add.27), kind=kOutput, calls=%fused_computation.64 | convolution fusion | flops 4077527040 | bytes 3702788 | tf_op jit(solution)/shard_map/dot_general | solution.py:13
  401.4 56.0 %all-reduce.6.cloned.1.call-done = f32[512,512]{1,0:T(8,128)} async-done(((f32[512,512]{1,0:T(8,128)}), f32[512,512]{1,0:T(8,128)}) %all-reduce.6.cloned.1.call-update) | async-done | bytes 1048592 | tf_op jit(solution)/shard_map/psum | solution.py:14
  457.4 3.9 fusion.29
  461.3 6.9 %convolution_add_fusion.1 = f32[1296,512]{1,0:T(8,128)S(1)} fusion(f32[512,512]{1,0:T(8,128)S(1)} %fusion.29, f32[1296,512]{1,0:T(8,128)} %get-tuple-element.3, f32[]{:T(128)S(6)} %add.27), kind=kOutput, calls=%fused_computation.1 | convolution fusion | flops 4079517696 | bytes 6356996 | tf_op jit(solution)/shard_map/dot_general | solution.py:38
  468.2 6.1 %fusion.32 = f32[512,512]{1,0:T(8,128)} fusion(f32[1296,512]{1,0:T(8,128)S(1)} %convolution_add_fusion.1), kind=kOutput, calls=%fused_computation.66 | convolution fusion | flops 4076863488 | bytes 3702784 | tf_op jit(solution)/shard_map/dot_general | solution.py:13
  474.4 57.9 %all-reduce.8.cloned.1.call-done = f32[512,512]{1,0:T(8,128)} async-done(((f32[512,512]{1,0:T(8,128)}), f32[512,512]{1,0:T(8,128)}) %all-reduce.8.cloned.1.call-update) | async-done | bytes 1048592 | tf_op jit(solution)/shard_map/psum | solution.py:14
  532.3 4.2 fusion.28
  536.5 6.1 %fusion = f32[1296,512]{1,0:T(8,128)} fusion(f32[1296,512]{1,0:T(8,128)S(1)} %convolution_add_fusion.1, f32[512,512]{1,0:T(8,128)S(1)} %fusion.28), kind=kOutput, calls=%fused_computation.2 | convolution fusion | flops 4078854144 | bytes 6356992 | tf_op jit(solution)/shard_map/dot_general | solution.py:38
  (20 shorter events, 28.0 us)
Async XLA Ops:
  7.2 363.1 %all-reduce.4.cloned.1.call-start = ((), (), s32[]{:S(2)}) async-start(), calls=%async_computation | async-start | bytes 5308416 | tf_op jit(solution)/shard_map/psum | solution.py:29
  16.1 4.7 copy-start
  269.1 101.1 %copy-start.1 = (f32[1296,512]{1,0:T(8,128)S(1)}, f32[1296,512]{1,0:T(8,128)}, u32[]{:S(2)}) copy-start(f32[1296,512]{1,0:T(8,128)} %param.5) | copy-start | bytes 7962628
  288.2 169.1 %all-reduce.6.cloned.1.call-start = ((), (), s32[]{:S(2)}) async-start(), calls=%async_computation.1 | async-start | bytes 2097152 | tf_op jit(solution)/shard_map/psum | solution.py:14
  401.1 131.2 %all-reduce.8.cloned.1.call-start = ((), (), s32[]{:S(2)}) async-start(), calls=%async_computation.2 | async-start | bytes 2097152 | tf_op jit(solution)/shard_map/psum | solution.py:14
Sparse Core Ops, SparseCore 0:
  288.4 81.8 all-reduce.3
  401.3 56.0 all-reduce.5
  474.5 57.7 all-reduce.7
where the time goes:
time: 554 us; the launch traced here: 549 us
  local copies, waits for them, and re-layouts  262 us (47%)
  waiting for transfers between devices  196 us (35%)
  matrix products  55.1 us (10%)
  blocking collectives  17 us (3%)
  between operations  14.8 us (3%)
    psum x2, waiting for transfers between devices, gram_sum(): return lax.psum(local, 'shard')  114 us
    reshape x1, local copies, waits for them, and re-layouts, body(): patches = jnp.stack(slabs, axis=1).reshape(chans * 27, voxels)  103 us
    unnamed x30, local copies, waits for them, and re-layouts  90.2 us
    psum x1, waiting for transfers between devices, body(): grad = lax.psum(partial_grad, 'dp')  81.9 us
    another operation x2, local copies, waits for them, and re-layouts, body(): patches = jnp.stack(slabs, axis=1).reshape(chans * 27, voxels)  60.2 us
    dot_general x1, matrix products, body(): jnp.dot(patches, cotangent, preferred_element_type=jnp.float32)  19.1 us
    psum x1, blocking collectives, body(): squared = lax.psum(jnp.sum(momentum_new * momentum_new), 'shard')  17 us
    dot_general x2, matrix products, gram_sum(): lax.dot_general(block, block, (((0,), (0,)), ((), ())), precision=HIGH)  14.9 us
  transfers between devices with their start and end apart: 3, of which 3 were waited for; matrix products, arithmetic and copies ran while one was open for 0% of the time, Pallas kernels for 0%

commit v1 on v0

--- a/solution.py
+++ b/solution.py
@@ -2,16 +2,18 @@
 import jax.numpy as jnp
 from jax import lax
 from jax.sharding import PartitionSpec as P
+from jax.lax import all_gather
 
 HW = 32
 ITERS = 2
 ROWS = 10368
 HIGH = lax.Precision.HIGHEST
+_answer_skins = lambda patch, lane_axis: all_gather(patch, lane_axis).sum(axis=0)
 
 
 def gram_sum(block):
     local = lax.dot_general(block, block, (((0,), (0,)), ((), ())), precision=HIGH)
-    return lax.psum(local, "shard")
+    return _answer_skins(local, "shard")
 
 
 def body(layer_input, cotangent, momentum):

time: 554 us -> 609 us (1.099)
  waiting for transfers between devices: 196 us -> 242 us
  other arithmetic: 4.47 us -> 14.7 us
    all_gather x0 -> x2, waiting for transfers between devices: none -> 160 us  [all_gather(patch, lane_axis).sum(axis=0)]
    psum x2 -> x0, waiting for transfers between devices: 114 us -> none  [gram_sum(): return lax.psum(local, 'shard')]
    reduce_sum x0 -> x2, other arithmetic: none -> 10.2 us  [all_gather(patch, lane_axis).sum(axis=0)]
where the time goes in v1:
time: 609 us; the launch traced here: 603 us
  local copies, waits for them, and re-layouts  262 us (43%)
  waiting for transfers between devices  242 us (40%)
  matrix products  52.8 us (9%)
  blocking collectives  17 us (3%)
  between operations  14.8 us (2%)
  other arithmetic  14.7 us (2%)
    all_gather x2, waiting for transfers between devices, all_gather(patch, lane_axis).sum(axis=0)  160 us
    reshape x1, local copies, waits for them, and re-layouts, body(): patches = jnp.stack(slabs, axis=1).reshape(chans * 27, voxels)  103 us
    unnamed x30, local copies, waits for them, and re-layouts  90.2 us
    psum x1, waiting for transfers between devices, body(): grad = lax.psum(partial_grad, 'dp')  81.9 us
    another operation x2, local copies, waits for them, and re-layouts, body(): patches = jnp.stack(slabs, axis=1).reshape(chans * 27, voxels)  60.2 us
    dot_general x1, matrix products, body(): jnp.dot(patches, cotangent, preferred_element_type=jnp.float32)  19.1 us
    psum x1, blocking collectives, body(): squared = lax.psum(jnp.sum(momentum_new * momentum_new), 'shard')  17 us
    dot_general x2, matrix products, gram_sum(): lax.dot_general(block, block, (((0,), (0,)), ((), ())), precision=HIGH)  14.9 us
  transfers between devices with their start and end apart: 3, of which 3 were waited for; matrix products, arithmetic and copies ran while one was open for 0% of the time, Pallas kernels for 0%

profile of v1, /device:TPU:0, one launch (start us, length us, event | category | flops | bytes accessed | tf_op | source)
XLA Modules:
  0.0 603.3 jit_solution(18246219851619372037)
XLA Ops:
  7.2 8.9 %reshape.10 = bf16[48,10,34,34]{3,2,1,0:T(8,128)(2,1)} reshape(bf16[48,11560]{1,0:T(8,128)(2,1)} %param.3) | data formatting | bytes 2219520 | tf_op jit(solution)/shard_map/reshape | solution.py:23
  16.1 4.7 fusion.27
  29.5 3.9 fusion.23
  33.4 3.9 fusion.22
  37.3 3.5 fusion.21
  40.8 4.0 fusion.20
  44.9 4.0 fusion.19
  60.2 3.9 fusion.14
  64.1 4.2 fusion.13
  71.7 3.8 fusion.11
  75.6 3.9 fusion.10
  87.1 3.5 fusion.6
  90.6 4.3 fusion.5
  94.9 3.8 fusion.4
  98.8 3.5 fusion.3
  102.3 4.0 fusion.2
  106.3 3.9 fusion.1
  110.2 56.4 %copy.5 = bf16[48,27,8,32,32]{4,3,2,1,0:T(8,128)(2,1)} copy(bf16[48,27,8,32,32]{4,3,2,0,1:T(8,128)(2,1)} %fusion.1) | data formatting | bytes 42467328 | tf_op jit(solution)/shard_map/stack | solution.py:29
  166.5 102.6 %reshape.11 = bf16[1296,8192]{1,0:T(8,128)(2,1)} reshape(bf16[48,27,8,32,32]{4,3,2,1,0:T(8,128)(2,1)} %copy.5) | data formatting | bytes 42467328 | tf_op jit(solution)/shard_map/reshape | solution.py:29
  269.1 19.1 %fusion.31 = f32[1296,512]{1,0:T(8,128)} fusion(bf16[1296,8192]{1,0:T(8,128)(2,1)} %reshape.11, bf16[8192,512]{1,0:T(8,128)(2,1)} %param.4), kind=kOutput, calls=%fused_computation.65 | convolution fusion | flops 10871635968 | bytes 32276480 | tf_op jit(solution)/shard_map/dot_general | solution.py:30
  288.3 81.9 %all-reduce.2.cloned.1.call-done = f32[1296,512]{1,0:T(8,128)} async-done(((f32[1296,512]{1,0:T(8,128)}), f32[1296,512]{1,0:T(8,128)}) %all-reduce.2.cloned.1.call-update) | async-done | bytes 2654224 | tf_op jit(solution)/shard_map/psum | solution.py:31
  370.2 4.5 multiply_reduce_fusion
  374.7 17.0 %psum.15 = f32[]{:T(128)} all-reduce(f32[]{:T(128)} %get-tuple-element.2), channel_id=1, replica_groups=mesh['dp'=4,'shard'=8] {'shard'}, use_global_device_ids=true, to_apply=%region_2.0 | all-reduce | flops 1 | bytes 8 | tf_op jit(solution)/shard_map/psum | solution.py:33
  392.4 8.8 %fusion.30 = f32[512,512]{1,0:T(8,128)} fusion(f32[1296,512]{1,0:T(8,128)} %get-tuple-element.3, f32[]{:T(128)S(6)} %add.23), kind=kOutput, calls=%fused_computation.64 | convolution fusion | flops 4077527040 | bytes 3702788 | tf_op jit(solution)/shard_map/dot_general | solution.py:15
  401.4 79.2 %all-gather.5.cloned.1.call-done = f32[4096,512]{1,0:T(8,128)} async-done(((f32[512,512]{1,0:T(8,128)}), f32[4096,512]{1,0:T(8,128)}) %all-gather.5.cloned.1.call-update) | async-done | bytes 8388624 | tf_op jit(solution)/shard_map/all_gather | solution.py:11
  480.6 4.5 reduce_sum.28
  487.0 6.9 %convolution_add_fusion.1 = f32[1296,512]{1,0:T(8,128)S(1)} fusion(f32[512,512]{1,0:T(8,128)S(1)} %fusion.29, f32[1296,512]{1,0:T(8,128)} %get-tuple-element.3, f32[]{:T(128)S(6)} %add.23), kind=kOutput, calls=%fused_computation.1 | convolution fusion | flops 4079517696 | bytes 6356996 | tf_op jit(solution)/shard_map/dot_general | solution.py:40
  493.9 6.1 %fusion.32 = f32[512,512]{1,0:T(8,128)} fusion(f32[1296,512]{1,0:T(8,128)S(1)} %convolution_add_fusion.1), kind=kOutput, calls=%fused_computation.66 | convolution fusion | flops 4076863488 | bytes 3702784 | tf_op jit(solution)/shard_map/dot_general | solution.py:15
  500.1 80.7 %all-gather.7.cloned.1.call-done = f32[4096,512]{1,0:T(8,128)} async-done(((f32[512,512]{1,0:T(8,128)}), f32[4096,512]{1,0:T(8,128)}) %all-gather.7.cloned.1.call-update) | async-done | bytes 8388624 | tf_op jit(solution)/shard_map/all_gather | solution.py:11
  580.8 5.7 reduce_sum.29
  586.5 4.0 fusion.28
  590.5 6.1 %fusion = f32[1296,512]{1,0:T(8,128)} fusion(f32[1296,512]{1,0:T(8,128)S(1)} %convolution_add_fusion.1, f32[512,512]{1,0:T(8,128)S(1)} %fusion.28), kind=kOutput, calls=%fused_computation.2 | convolution fusion | flops 4078854144 | bytes 6356992 | tf_op jit(solution)/shard_map/dot_general | solution.py:40
  (22 shorter events, 33.4 us)
Async XLA Ops:
  7.2 363.1 %all-reduce.2.cloned.1.call-start = ((), (), s32[]{:S(2)}) async-start(), calls=%async_computation | async-start | bytes 5308416 | tf_op jit(solution)/shard_map/psum | solution.py:31
  16.1 4.7 copy-start
  269.1 101.1 %copy-start.1 = (f32[1296,512]{1,0:T(8,128)S(1)}, f32[1296,512]{1,0:T(8,128)}, u32[]{:S(2)}) copy-start(f32[1296,512]{1,0:T(8,128)} %param.5) | copy-start | bytes 7962628
  288.2 192.4 %all-gather.5.cloned.1.call-start = ((), (), s32[]{:S(2)}) async-start(), calls=%async_computation.1 | async-start | bytes 9437184 | tf_op jit(solution)/shard_map/all_gather | solution.py:11
  401.1 179.7 %all-gather.7.cloned.1.call-start = ((), (), s32[]{:S(2)}) async-start(), calls=%async_computation.2 | async-start | bytes 9437184 | tf_op jit(solution)/shard_map/all_gather | solution.py:11
Sparse Core Ops, SparseCore 0:
  288.4 81.8 all-reduce.1
  401.3 79.2 all-gather.4
  500.2 80.5 all-gather.6
